TPU v7x, 256 devices: a whole 4x4x8 slice. The times are simulated.
256 devices in a mesh: leaf: 64 (over z, x, core), sub: 4 (over y).
Axes of the slice: x: 4, y: 4, z: 8, core: 2. Of those that a mesh axis runs over, the one named last changes fastest.
Arguments:
- coords: bfloat16 [32768, 3, 128], P('leaf'), may hold values from 0 to 4
- charges: bfloat16 [32768, 8, 128], P(('leaf', 'sub')), may hold values from -6 to 6
- counts: int32 [32768], P('leaf'), may hold values from 32 to 128, as said below
- morton: int32 [32768], P('leaf'), may hold values from 0 to 511, as said below
- near_list: int32 [32768, 27], P(('leaf', 'sub')), may hold values from -1 to 32767, as said below
- basis: bfloat16 [32768, 64, 128], P(('leaf', 'sub')), may hold values from -0.5 to 0.5
- transfer1: bfloat16 [32768, 64, 64], P(('leaf', 'sub')), may hold values from -0.75 to 0.75
- far2_list: int32 [4096, 16], P(('leaf', 'sub')), may hold values from -1 to 4095, as said below
- coupling2: bfloat16 [4096, 16, 64, 64], P(('leaf', 'sub')), may hold values from -0.0625 to 0.0625
- transfer2: bfloat16 [4096, 64, 64], P('leaf'), may hold values from -0.75 to 0.75
- far3_list: int32 [64, 8], P('leaf'), may hold values from -1 to 63, as said below
- coupling3: bfloat16 [64, 8, 64, 64], P('leaf'), may hold values from -0.01171875 to 0.01171875
Outputs:
- potential: float32 [32768, 8, 128], P(('leaf', 'sub'))
Inputs may be any that keep to these rules, and one draw needn't show every extreme that they name: `counts`: each leaf's number of live points; leaves do not all have the same number. `morton`: within every block of 512 consecutive entries, a permutation of 0 to 511. `near_list`: row t starts with t itself; its other live entries are leaves other than t in the leaf group of t or in the group just before or after it; live entries come first and -1 fills the rest, with at least 13 live entries a row; entries may repeat. `far2_list`: row b names boxes other than b in the leaf group of b or in the group just before or after it; live entries come first and -1 fills the rest, with at least 8 live entries a row; entries may repeat. `far3_list`: row q names group boxes other than q; live entries come first and -1 fills the rest, with at least 4 live entries a row; entries may repeat.
All inputs are finite; a program needn't handle non-finite values.
Results may differ from a plain program's by a relative error of at most 0.011.
Values may be sent and summed in bfloat16 or wider, within the bound.
No kernel may reach another device: no remote copies, remote signals or barrier semaphores. Data moves between devices by JAX's collectives and lax.ppermute only.
A program may use at most 64 MiB of HBM per device.

v0:
```python
import jax
import jax.numpy as jnp
from jax import lax
from jax.sharding import PartitionSpec as P

kernel_scale = 0.07957747154594767
delta_squared = 0.0025


def with_halo(cells, sides, width):
    for axis, dim in sides:
        count = lax.axis_size(axis)
        ends = count - 1
        head = lax.slice_in_dim(cells, 0, width, axis=dim)
        tail = lax.slice_in_dim(cells, cells.shape[dim] - width, cells.shape[dim], axis=dim)
        cells = jnp.concatenate(
            [
                lax.ppermute(tail, axis, [(i, (i + 1) % count) for i in range(ends)]),
                cells,
                lax.ppermute(head, axis, [((i + 1) % count, i) for i in range(ends)]),
            ],
            axis=dim,
        )
    return cells


def kernel_tile(targets, sources):
    squared = jnp.zeros((targets.shape[0], targets.shape[2], sources.shape[2]), jnp.float32)
    for component in range(3):
        offset = targets[:, component, :, None] - sources[:, component, None, :]
        squared = squared + offset * offset
    return (kernel_scale / jnp.sqrt(squared + delta_squared)).astype(jnp.bfloat16)


def far_field(moments, lists, couplings, offset):
    valid = lists >= 0
    local = jnp.clip(lists - offset, 0, moments.shape[0] - 1)
    source = jnp.where(valid[..., None, None], moments[local], jnp.zeros((), moments.dtype))
    return jnp.einsum("bkrc,bkcp->brp", source, couplings, preferred_element_type=jnp.float32)


def on_device(
    coords,
    charges,
    counts,
    morton,
    near_list,
    basis,
    transfer1,
    far2_list,
    coupling2,
    transfer2,
    far3_list,
    coupling3,
):
    lane = lax.axis_index("sub")
    group = lax.axis_index("leaf")
    leaf_dev = charges.shape[0]
    rhs_count = charges.shape[1]
    points = charges.shape[2]
    rank_size = basis.shape[1]
    group_size = coords.shape[0]
    clusters = far2_list.shape[0]
    group_boxes = transfer2.shape[0]
    start = lane * leaf_dev
    arrived = lax.all_gather(charges, "sub", axis=0, tiled=True)
    inverse = (
        jnp.zeros((group_size,), jnp.int32).at[morton].set(jnp.arange(group_size, dtype=jnp.int32))
    )
    ordered = arrived[inverse]
    live = jnp.arange(points, dtype=jnp.int32)[None, :] < counts[:, None]
    masked = jnp.where(live[:, None, :], ordered, jnp.zeros((), ordered.dtype))
    packed = jnp.concatenate([coords, masked], axis=1)
    nearby = with_halo(packed, (("leaf", 0),), group_size)
    own_charges = lax.dynamic_slice_in_dim(masked, start, leaf_dev, 0)
    own_live = lax.dynamic_slice_in_dim(live, start, leaf_dev, 0)
    targets = lax.dynamic_slice_in_dim(coords, start, leaf_dev, 0).astype(jnp.float32)
    transfer_boxed = transfer1.reshape(clusters, 8, rank_size, rank_size)
    leaf_moments = jnp.einsum(
        "trp,tkp->trk", own_charges, basis, preferred_element_type=jnp.float32
    ).astype(jnp.bfloat16)
    box_moments = jnp.einsum(
        "bnrc,bncp->brp",
        leaf_moments.reshape(clusters, 8, rhs_count, rank_size),
        transfer_boxed,
        preferred_element_type=jnp.float32,
    ).astype(jnp.bfloat16)
    group_moments = lax.all_gather(box_moments, "sub", axis=0, tiled=True)
    top_moment = jnp.einsum(
        "brc,bcp->rp", group_moments, transfer2, preferred_element_type=jnp.float32
    ).astype(jnp.bfloat16)
    all_top = lax.all_gather(top_moment[None], "leaf", axis=0, tiled=True)
    near_boxes = with_halo(group_moments, (("leaf", 0),), group_boxes)
    top_field = far_field(all_top, far3_list, coupling3, 0).astype(jnp.bfloat16)
    box_far = far_field(near_boxes, far2_list, coupling2, (group - 1) * group_boxes)
    own_transfer = lax.dynamic_slice_in_dim(transfer2, lane * clusters, clusters, 0)
    box_local = (
        box_far
        + jnp.einsum("rp,bcp->brc", top_field[0], own_transfer, preferred_element_type=jnp.float32)
    ).astype(jnp.bfloat16)
    leaf_local = jnp.einsum(
        "brp,bncp->bnrc", box_local, transfer_boxed, preferred_element_type=jnp.float32
    ).astype(jnp.bfloat16)
    leaf_local = leaf_local.reshape(leaf_dev, rhs_count, rank_size)
    far_part = jnp.einsum("trk,tkp->trp", leaf_local, basis, preferred_element_type=jnp.float32)
    base = (group - 1) * group_size

    def slot_step(total, column):
        valid = column >= 0
        index = jnp.clip(column - base, 0, 3 * group_size - 1)
        rows = nearby[index]
        tile = kernel_tile(targets, rows[:, :3].astype(jnp.float32))
        source = jnp.where(valid[:, None, None], rows[:, 3:], jnp.zeros((), rows.dtype))
        return (
            total + jnp.einsum("tij,trj->tri", tile, source, preferred_element_type=jnp.float32),
            None,
        )

    near_part, unused = lax.scan(
        slot_step, jnp.zeros((leaf_dev, rhs_count, points), jnp.float32), near_list.T
    )
    return jnp.where(own_live[:, None, :], near_part + far_part, jnp.zeros((), jnp.float32))


def solution(mesh):
    return jax.shard_map(
        on_device,
        mesh=mesh,
        in_specs=(
            P("leaf", None, None),
            P(("leaf", "sub"), None, None),
            P("leaf"),
            P("leaf"),
            P(("leaf", "sub"), None),
            P(("leaf", "sub"), None, None),
            P(("leaf", "sub"), None, None),
            P(("leaf", "sub"), None),
            P(("leaf", "sub"), None, None, None),
            P("leaf", None, None),
            P("leaf", None),
            P("leaf", None, None, None),
        ),
        out_specs=P(("leaf", "sub"), None, None),
        check_vma=False,
    )
```

profile of v0, /device:TPU:1, one launch (start us, length us, event | category | flops | bytes accessed | tf_op | source)
XLA Modules:
  0.0 683.8 jit_solution(16244068060757462938)
XLA Ops:
  19.3 19.4 %all-gather.3.cloned.1.call-done = bf16[512,8,128]{2,1,0:T(8,128)(2,1)} async-done(((bf16[128,8,128]{2,1,0:T(8,128)(2,1)}), bf16[512,8,128]{2,1,0:T(8,128)(2,1)}) %all-gather.3.cloned.1.call-update) | async-done | bytes 1048592 | tf_op jit(solution)/shard_map/all_gather | solution.py:66
  45.3 9.5 %all_gather.10 = bf16[64,8,64]{2,1,0:T(8,128)(2,1)S(1)} all-gather(bf16[16,8,64]{2,1,0:T(8,128)(2,1)S(1)} %fusion.10), channel_id=1, replica_groups=mesh['leaf'=64,'sub'=4] {'sub'}, dimensions={0}, use_global_device_ids=true | all-gather | bytes 81920 | tf_op jit(solution)/shard_map/all_gather | solution.py:88
  72.1 72.7 %all-gather = bf16[512,64]{1,0:T(8,128)(2,1)} all-gather(bf16[8,64]{1,0:T(8,128)(2,1)S(1)} %fusion.12), channel_id=2, replica_groups=mesh['leaf'=64,'sub'=4] {'leaf'}, dimensions={0}, use_global_device_ids=true | all-gather | bytes 66560 | tf_op jit(solution)/shard_map/all_gather | solution.py:92
  167.0 25.8 %pad_maximum_fusion = bf16[1536,11,128]{2,1,0:T(8,128)(2,1)} fusion(bf16[512,11,128]{2,1,0:T(8,128)(2,1)S(1)} %copy.22, bf16[512,8,128]{2,1,0:T(8,128)(2,1)S(1)} %broadcast_select_fusion, bf16[512,3,128]{2,1,0:T(4,128)(2,1)S(1)} %copy-done.3, bf16[512,11,128]{2,1,0:T(8,128)(2,1)S(1)} %copy.21), kind=kLoop, calls=%fused_computation.23 | loop fusion | flops 17301504 | bytes 8650752 | tf_op jit(solution)/shard_map/concatenate | solution.py:16
  192.7 482.2 %while.11 = (s32[]{:T(128)}, f32[128,8,128]{2,1,0:T(8,128)}, s32[27,128]{1,0:T(8,128)}, s32[]{:T(128)}, bf16[1536,11,128]{2,1,0:T(8,128)(2,1)}, /*index=5*/f32[128,3,128]{2,0,1:T(8,128)S(1)}, s32[]{:T(128)}, s32[]{:T(128)}) while((s32[]{:T(128)}, f32[128,8,128]{2,1,0:T(8,128)}, s32[27,128]{1,0:T(8,128)}, s32[]{:T(128)}, ...), condition=%wide.region_2.3_spmd.clone, body=%wide.region_1.2_spmd.clone.sunk | while | flops 57067264 | bytes 3513195 | solution.py:119
  199.1 11.5 %fusion.50 = f32[128,8,128]{2,1,0:T(8,128)} fusion(f32[128,128]{1,0:T(8,128)S(1)} %bitcast.93, f32[128,128]{1,0:T(8,128)} %get-tuple-element.121, f32[128,128]{1,0:T(8,128)S(1)} %bitcast.94, f32[128,128]{1,0:T(8,128)} %get-tuple-element.123, f32[128,128]{1,0:T(8,128)S(1)} %bitcast.92, f32[128,128]{1,0:T(8,128)} %get-tuple-element.125, ...), kind=kOutput, calls=%fused_computation.7.clone.1 | convolution fusion | flops 57016320 | bytes 1704065 | tf_op jit(solution)/shard_map/while/body/eval_jaxpr/tij,trj->tri/dot_general | solution.py:115
  216.9 11.6 %fusion.50 = f32[128,8,128]{2,1,0:T(8,128)} fusion(f32[128,128]{1,0:T(8,128)S(1)} %bitcast.93, f32[128,128]{1,0:T(8,128)} %get-tuple-element.121, f32[128,128]{1,0:T(8,128)S(1)} %bitcast.94, f32[128,128]{1,0:T(8,128)} %get-tuple-element.123, f32[128,128]{1,0:T(8,128)S(1)} %bitcast.92, f32[128,128]{1,0:T(8,128)} %get-tuple-element.125, ...), kind=kOutput, calls=%fused_computation.7.clone.1 | convolution fusion | flops 57016320 | bytes 1704065 | tf_op jit(solution)/shard_map/while/body/eval_jaxpr/tij,trj->tri/dot_general | solution.py:115
  234.7 11.6 %fusion.50 = f32[128,8,128]{2,1,0:T(8,128)} fusion(f32[128,128]{1,0:T(8,128)S(1)} %bitcast.93, f32[128,128]{1,0:T(8,128)} %get-tuple-element.121, f32[128,128]{1,0:T(8,128)S(1)} %bitcast.94, f32[128,128]{1,0:T(8,128)} %get-tuple-element.123, f32[128,128]{1,0:T(8,128)S(1)} %bitcast.92, f32[128,128]{1,0:T(8,128)} %get-tuple-element.125, ...), kind=kOutput, calls=%fused_computation.7.clone.1 | convolution fusion | flops 57016320 | bytes 1704065 | tf_op jit(solution)/shard_map/while/body/eval_jaxpr/tij,trj->tri/dot_general | solution.py:115
  252.6 11.6 %fusion.50 = f32[128,8,128]{2,1,0:T(8,128)} fusion(f32[128,128]{1,0:T(8,128)S(1)} %bitcast.93, f32[128,128]{1,0:T(8,128)} %get-tuple-element.121, f32[128,128]{1,0:T(8,128)S(1)} %bitcast.94, f32[128,128]{1,0:T(8,128)} %get-tuple-element.123, f32[128,128]{1,0:T(8,128)S(1)} %bitcast.92, f32[128,128]{1,0:T(8,128)} %get-tuple-element.125, ...), kind=kOutput, calls=%fused_computation.7.clone.1 | convolution fusion | flops 57016320 | bytes 1704065 | tf_op jit(solution)/shard_map/while/body/eval_jaxpr/tij,trj->tri/dot_general | solution.py:115
  270.5 11.6 %fusion.50 = f32[128,8,128]{2,1,0:T(8,128)} fusion(f32[128,128]{1,0:T(8,128)S(1)} %bitcast.93, f32[128,128]{1,0:T(8,128)} %get-tuple-element.121, f32[128,128]{1,0:T(8,128)S(1)} %bitcast.94, f32[128,128]{1,0:T(8,128)} %get-tuple-element.123, f32[128,128]{1,0:T(8,128)S(1)} %bitcast.92, f32[128,128]{1,0:T(8,128)} %get-tuple-element.125, ...), kind=kOutput, calls=%fused_computation.7.clone.1 | convolution fusion | flops 57016320 | bytes 1704065 | tf_op jit(solution)/shard_map/while/body/eval_jaxpr/tij,trj->tri/dot_general | solution.py:115
  288.3 11.6 %fusion.50 = f32[128,8,128]{2,1,0:T(8,128)} fusion(f32[128,128]{1,0:T(8,128)S(1)} %bitcast.93, f32[128,128]{1,0:T(8,128)} %get-tuple-element.121, f32[128,128]{1,0:T(8,128)S(1)} %bitcast.94, f32[128,128]{1,0:T(8,128)} %get-tuple-element.123, f32[128,128]{1,0:T(8,128)S(1)} %bitcast.92, f32[128,128]{1,0:T(8,128)} %get-tuple-element.125, ...), kind=kOutput, calls=%fused_computation.7.clone.1 | convolution fusion | flops 57016320 | bytes 1704065 | tf_op jit(solution)/shard_map/while/body/eval_jaxpr/tij,trj->tri/dot_general | solution.py:115
  306.2 11.6 %fusion.50 = f32[128,8,128]{2,1,0:T(8,128)} fusion(f32[128,128]{1,0:T(8,128)S(1)} %bitcast.93, f32[128,128]{1,0:T(8,128)} %get-tuple-element.121, f32[128,128]{1,0:T(8,128)S(1)} %bitcast.94, f32[128,128]{1,0:T(8,128)} %get-tuple-element.123, f32[128,128]{1,0:T(8,128)S(1)} %bitcast.92, f32[128,128]{1,0:T(8,128)} %get-tuple-element.125, ...), kind=kOutput, calls=%fused_computation.7.clone.1 | convolution fusion | flops 57016320 | bytes 1704065 | tf_op jit(solution)/shard_map/while/body/eval_jaxpr/tij,trj->tri/dot_general | solution.py:115
  324.1 11.6 %fusion.50 = f32[128,8,128]{2,1,0:T(8,128)} fusion(f32[128,128]{1,0:T(8,128)S(1)} %bitcast.93, f32[128,128]{1,0:T(8,128)} %get-tuple-element.121, f32[128,128]{1,0:T(8,128)S(1)} %bitcast.94, f32[128,128]{1,0:T(8,128)} %get-tuple-element.123, f32[128,128]{1,0:T(8,128)S(1)} %bitcast.92, f32[128,128]{1,0:T(8,128)} %get-tuple-element.125, ...), kind=kOutput, calls=%fused_computation.7.clone.1 | convolution fusion | flops 57016320 | bytes 1704065 | tf_op jit(solution)/shard_map/while/body/eval_jaxpr/tij,trj->tri/dot_general | solution.py:115
  341.9 11.6 %fusion.50 = f32[128,8,128]{2,1,0:T(8,128)} fusion(f32[128,128]{1,0:T(8,128)S(1)} %bitcast.93, f32[128,128]{1,0:T(8,128)} %get-tuple-element.121, f32[128,128]{1,0:T(8,128)S(1)} %bitcast.94, f32[128,128]{1,0:T(8,128)} %get-tuple-element.123, f32[128,128]{1,0:T(8,128)S(1)} %bitcast.92, f32[128,128]{1,0:T(8,128)} %get-tuple-element.125, ...), kind=kOutput, calls=%fused_computation.7.clone.1 | convolution fusion | flops 57016320 | bytes 1704065 | tf_op jit(solution)/shard_map/while/body/eval_jaxpr/tij,trj->tri/dot_general | solution.py:115
  359.8 11.6 %fusion.50 = f32[128,8,128]{2,1,0:T(8,128)} fusion(f32[128,128]{1,0:T(8,128)S(1)} %bitcast.93, f32[128,128]{1,0:T(8,128)} %get-tuple-element.121, f32[128,128]{1,0:T(8,128)S(1)} %bitcast.94, f32[128,128]{1,0:T(8,128)} %get-tuple-element.123, f32[128,128]{1,0:T(8,128)S(1)} %bitcast.92, f32[128,128]{1,0:T(8,128)} %get-tuple-element.125, ...), kind=kOutput, calls=%fused_computation.7.clone.1 | convolution fusion | flops 57016320 | bytes 1704065 | tf_op jit(solution)/shard_map/while/body/eval_jaxpr/tij,trj->tri/dot_general | solution.py:115
  377.6 11.6 %fusion.50 = f32[128,8,128]{2,1,0:T(8,128)} fusion(f32[128,128]{1,0:T(8,128)S(1)} %bitcast.93, f32[128,128]{1,0:T(8,128)} %get-tuple-element.121, f32[128,128]{1,0:T(8,128)S(1)} %bitcast.94, f32[128,128]{1,0:T(8,128)} %get-tuple-element.123, f32[128,128]{1,0:T(8,128)S(1)} %bitcast.92, f32[128,128]{1,0:T(8,128)} %get-tuple-element.125, ...), kind=kOutput, calls=%fused_computation.7.clone.1 | convolution fusion | flops 57016320 | bytes 1704065 | tf_op jit(solution)/shard_map/while/body/eval_jaxpr/tij,trj->tri/dot_general | solution.py:115
  395.5 11.6 %fusion.50 = f32[128,8,128]{2,1,0:T(8,128)} fusion(f32[128,128]{1,0:T(8,128)S(1)} %bitcast.93, f32[128,128]{1,0:T(8,128)} %get-tuple-element.121, f32[128,128]{1,0:T(8,128)S(1)} %bitcast.94, f32[128,128]{1,0:T(8,128)} %get-tuple-element.123, f32[128,128]{1,0:T(8,128)S(1)} %bitcast.92, f32[128,128]{1,0:T(8,128)} %get-tuple-element.125, ...), kind=kOutput, calls=%fused_computation.7.clone.1 | convolution fusion | flops 57016320 | bytes 1704065 | tf_op jit(solution)/shard_map/while/body/eval_jaxpr/tij,trj->tri/dot_general | solution.py:115
  413.4 11.6 %fusion.50 = f32[128,8,128]{2,1,0:T(8,128)} fusion(f32[128,128]{1,0:T(8,128)S(1)} %bitcast.93, f32[128,128]{1,0:T(8,128)} %get-tuple-element.121, f32[128,128]{1,0:T(8,128)S(1)} %bitcast.94, f32[128,128]{1,0:T(8,128)} %get-tuple-element.123, f32[128,128]{1,0:T(8,128)S(1)} %bitcast.92, f32[128,128]{1,0:T(8,128)} %get-tuple-element.125, ...), kind=kOutput, calls=%fused_computation.7.clone.1 | convolution fusion | flops 57016320 | bytes 1704065 | tf_op jit(solution)/shard_map/while/body/eval_jaxpr/tij,trj->tri/dot_general | solution.py:115
  431.2 11.6 %fusion.50 = f32[128,8,128]{2,1,0:T(8,128)} fusion(f32[128,128]{1,0:T(8,128)S(1)} %bitcast.93, f32[128,128]{1,0:T(8,128)} %get-tuple-element.121, f32[128,128]{1,0:T(8,128)S(1)} %bitcast.94, f32[128,128]{1,0:T(8,128)} %get-tuple-element.123, f32[128,128]{1,0:T(8,128)S(1)} %bitcast.92, f32[128,128]{1,0:T(8,128)} %get-tuple-element.125, ...), kind=kOutput, calls=%fused_computation.7.clone.1 | convolution fusion | flops 57016320 | bytes 1704065 | tf_op jit(solution)/shard_map/while/body/eval_jaxpr/tij,trj->tri/dot_general | solution.py:115
  449.1 11.6 %fusion.50 = f32[128,8,128]{2,1,0:T(8,128)} fusion(f32[128,128]{1,0:T(8,128)S(1)} %bitcast.93, f32[128,128]{1,0:T(8,128)} %get-tuple-element.121, f32[128,128]{1,0:T(8,128)S(1)} %bitcast.94, f32[128,128]{1,0:T(8,128)} %get-tuple-element.123, f32[128,128]{1,0:T(8,128)S(1)} %bitcast.92, f32[128,128]{1,0:T(8,128)} %get-tuple-element.125, ...), kind=kOutput, calls=%fused_computation.7.clone.1 | convolution fusion | flops 57016320 | bytes 1704065 | tf_op jit(solution)/shard_map/while/body/eval_jaxpr/tij,trj->tri/dot_general | solution.py:115
  467.0 11.6 %fusion.50 = f32[128,8,128]{2,1,0:T(8,128)} fusion(f32[128,128]{1,0:T(8,128)S(1)} %bitcast.93, f32[128,128]{1,0:T(8,128)} %get-tuple-element.121, f32[128,128]{1,0:T(8,128)S(1)} %bitcast.94, f32[128,128]{1,0:T(8,128)} %get-tuple-element.123, f32[128,128]{1,0:T(8,128)S(1)} %bitcast.92, f32[128,128]{1,0:T(8,128)} %get-tuple-element.125, ...), kind=kOutput, calls=%fused_computation.7.clone.1 | convolution fusion | flops 57016320 | bytes 1704065 | tf_op jit(solution)/shard_map/while/body/eval_jaxpr/tij,trj->tri/dot_general | solution.py:115
  484.8 11.6 %fusion.50 = f32[128,8,128]{2,1,0:T(8,128)} fusion(f32[128,128]{1,0:T(8,128)S(1)} %bitcast.93, f32[128,128]{1,0:T(8,128)} %get-tuple-element.121, f32[128,128]{1,0:T(8,128)S(1)} %bitcast.94, f32[128,128]{1,0:T(8,128)} %get-tuple-element.123, f32[128,128]{1,0:T(8,128)S(1)} %bitcast.92, f32[128,128]{1,0:T(8,128)} %get-tuple-element.125, ...), kind=kOutput, calls=%fused_computation.7.clone.1 | convolution fusion | flops 57016320 | bytes 1704065 | tf_op jit(solution)/shard_map/while/body/eval_jaxpr/tij,trj->tri/dot_general | solution.py:115
  502.7 11.6 %fusion.50 = f32[128,8,128]{2,1,0:T(8,128)} fusion(f32[128,128]{1,0:T(8,128)S(1)} %bitcast.93, f32[128,128]{1,0:T(8,128)} %get-tuple-element.121, f32[128,128]{1,0:T(8,128)S(1)} %bitcast.94, f32[128,128]{1,0:T(8,128)} %get-tuple-element.123, f32[128,128]{1,0:T(8,128)S(1)} %bitcast.92, f32[128,128]{1,0:T(8,128)} %get-tuple-element.125, ...), kind=kOutput, calls=%fused_computation.7.clone.1 | convolution fusion | flops 57016320 | bytes 1704065 | tf_op jit(solution)/shard_map/while/body/eval_jaxpr/tij,trj->tri/dot_general | solution.py:115
  520.5 11.6 %fusion.50 = f32[128,8,128]{2,1,0:T(8,128)} fusion(f32[128,128]{1,0:T(8,128)S(1)} %bitcast.93, f32[128,128]{1,0:T(8,128)} %get-tuple-element.121, f32[128,128]{1,0:T(8,128)S(1)} %bitcast.94, f32[128,128]{1,0:T(8,128)} %get-tuple-element.123, f32[128,128]{1,0:T(8,128)S(1)} %bitcast.92, f32[128,128]{1,0:T(8,128)} %get-tuple-element.125, ...), kind=kOutput, calls=%fused_computation.7.clone.1 | convolution fusion | flops 57016320 | bytes 1704065 | tf_op jit(solution)/shard_map/while/body/eval_jaxpr/tij,trj->tri/dot_general | solution.py:115
  538.4 11.6 %fusion.50 = f32[128,8,128]{2,1,0:T(8,128)} fusion(f32[128,128]{1,0:T(8,128)S(1)} %bitcast.93, f32[128,128]{1,0:T(8,128)} %get-tuple-element.121, f32[128,128]{1,0:T(8,128)S(1)} %bitcast.94, f32[128,128]{1,0:T(8,128)} %get-tuple-element.123, f32[128,128]{1,0:T(8,128)S(1)} %bitcast.92, f32[128,128]{1,0:T(8,128)} %get-tuple-element.125, ...), kind=kOutput, calls=%fused_computation.7.clone.1 | convolution fusion | flops 57016320 | bytes 1704065 | tf_op jit(solution)/shard_map/while/body/eval_jaxpr/tij,trj->tri/dot_general | solution.py:115
  556.3 11.6 %fusion.50 = f32[128,8,128]{2,1,0:T(8,128)} fusion(f32[128,128]{1,0:T(8,128)S(1)} %bitcast.93, f32[128,128]{1,0:T(8,128)} %get-tuple-element.121, f32[128,128]{1,0:T(8,128)S(1)} %bitcast.94, f32[128,128]{1,0:T(8,128)} %get-tuple-element.123, f32[128,128]{1,0:T(8,128)S(1)} %bitcast.92, f32[128,128]{1,0:T(8,128)} %get-tuple-element.125, ...), kind=kOutput, calls=%fused_computation.7.clone.1 | convolution fusion | flops 57016320 | bytes 1704065 | tf_op jit(solution)/shard_map/while/body/eval_jaxpr/tij,trj->tri/dot_general | solution.py:115
  574.1 11.6 %fusion.50 = f32[128,8,128]{2,1,0:T(8,128)} fusion(f32[128,128]{1,0:T(8,128)S(1)} %bitcast.93, f32[128,128]{1,0:T(8,128)} %get-tuple-element.121, f32[128,128]{1,0:T(8,128)S(1)} %bitcast.94, f32[128,128]{1,0:T(8,128)} %get-tuple-element.123, f32[128,128]{1,0:T(8,128)S(1)} %bitcast.92, f32[128,128]{1,0:T(8,128)} %get-tuple-element.125, ...), kind=kOutput, calls=%fused_computation.7.clone.1 | convolution fusion | flops 57016320 | bytes 1704065 | tf_op jit(solution)/shard_map/while/body/eval_jaxpr/tij,trj->tri/dot_general | solution.py:115
  592.0 11.6 %fusion.50 = f32[128,8,128]{2,1,0:T(8,128)} fusion(f32[128,128]{1,0:T(8,128)S(1)} %bitcast.93, f32[128,128]{1,0:T(8,128)} %get-tuple-element.121, f32[128,128]{1,0:T(8,128)S(1)} %bitcast.94, f32[128,128]{1,0:T(8,128)} %get-tuple-element.123, f32[128,128]{1,0:T(8,128)S(1)} %bitcast.92, f32[128,128]{1,0:T(8,128)} %get-tuple-element.125, ...), kind=kOutput, calls=%fused_computation.7.clone.1 | convolution fusion | flops 57016320 | bytes 1704065 | tf_op jit(solution)/shard_map/while/body/eval_jaxpr/tij,trj->tri/dot_general | solution.py:115
  609.8 11.6 %fusion.50 = f32[128,8,128]{2,1,0:T(8,128)} fusion(f32[128,128]{1,0:T(8,128)S(1)} %bitcast.93, f32[128,128]{1,0:T(8,128)} %get-tuple-element.121, f32[128,128]{1,0:T(8,128)S(1)} %bitcast.94, f32[128,128]{1,0:T(8,128)} %get-tuple-element.123, f32[128,128]{1,0:T(8,128)S(1)} %bitcast.92, f32[128,128]{1,0:T(8,128)} %get-tuple-element.125, ...), kind=kOutput, calls=%fused_computation.7.clone.1 | convolution fusion | flops 57016320 | bytes 1704065 | tf_op jit(solution)/shard_map/while/body/eval_jaxpr/tij,trj->tri/dot_general | solution.py:115
  627.7 11.6 %fusion.50 = f32[128,8,128]{2,1,0:T(8,128)} fusion(f32[128,128]{1,0:T(8,128)S(1)} %bitcast.93, f32[128,128]{1,0:T(8,128)} %get-tuple-element.121, f32[128,128]{1,0:T(8,128)S(1)} %bitcast.94, f32[128,128]{1,0:T(8,128)} %get-tuple-element.123, f32[128,128]{1,0:T(8,128)S(1)} %bitcast.92, f32[128,128]{1,0:T(8,128)} %get-tuple-element.125, ...), kind=kOutput, calls=%fused_computation.7.clone.1 | convolution fusion | flops 57016320 | bytes 1704065 | tf_op jit(solution)/shard_map/while/body/eval_jaxpr/tij,trj->tri/dot_general | solution.py:115
  645.6 11.6 %fusion.50 = f32[128,8,128]{2,1,0:T(8,128)} fusion(f32[128,128]{1,0:T(8,128)S(1)} %bitcast.93, f32[128,128]{1,0:T(8,128)} %get-tuple-element.121, f32[128,128]{1,0:T(8,128)S(1)} %bitcast.94, f32[128,128]{1,0:T(8,128)} %get-tuple-element.123, f32[128,128]{1,0:T(8,128)S(1)} %bitcast.92, f32[128,128]{1,0:T(8,128)} %get-tuple-element.125, ...), kind=kOutput, calls=%fused_computation.7.clone.1 | convolution fusion | flops 57016320 | bytes 1704065 | tf_op jit(solution)/shard_map/while/body/eval_jaxpr/tij,trj->tri/dot_general | solution.py:115
  663.4 11.6 %fusion.50 = f32[128,8,128]{2,1,0:T(8,128)} fusion(f32[128,128]{1,0:T(8,128)S(1)} %bitcast.93, f32[128,128]{1,0:T(8,128)} %get-tuple-element.121, f32[128,128]{1,0:T(8,128)S(1)} %bitcast.94, f32[128,128]{1,0:T(8,128)} %get-tuple-element.123, f32[128,128]{1,0:T(8,128)S(1)} %bitcast.92, f32[128,128]{1,0:T(8,128)} %get-tuple-element.125, ...), kind=kOutput, calls=%fused_computation.7.clone.1 | convolution fusion | flops 57016320 | bytes 1704065 | tf_op jit(solution)/shard_map/while/body/eval_jaxpr/tij,trj->tri/dot_general | solution.py:115
  (252 shorter events, 229.9 us)
Async XLA Ops:
  6.5 37.1 %copy-start = (bf16[128,64,128]{2,1,0:T(8,128)(2,1)S(1)}, bf16[128,64,128]{2,1,0:T(8,128)(2,1)}, u32[]{:S(2)}) copy-start(bf16[128,64,128]{2,1,0:T(8,128)(2,1)} %param.19) | copy-start | bytes 6291460
  6.5 12.7 %copy-start.6 = (s32[16,16]{1,0:T(8,128)S(1)}, s32[16,16]{1,0:T(8,128)}, u32[]{:S(2)}) copy-start(s32[16,16]{1,0:T(8,128)} %param.21) | copy-start | bytes 3076
  6.5 11.6 %copy-start.8 = (s32[1,8]{1,0:T(1,128)S(1)}, s32[1,8]{1,0:T(1,128)}, u32[]{:S(2)}) copy-start(s32[1,8]{1,0:T(1,128)} %param.24) | copy-start | bytes 100
  6.5 11.6 %copy-start.7 = (s32[512]{0:T(512)S(1)}, s32[512]{0:T(512)}, u32[]{:S(2)}) copy-start(s32[512]{0:T(512)} %param.16) | copy-start | bytes 6148
  6.5 32.1 %all-gather.3.cloned.1.call-start = ((), (), s32[]{:S(2)}) async-start(), calls=%async_computation | async-start | bytes 1310720 | tf_op jit(solution)/shard_map/all_gather | solution.py:66
  42.0 2.9 copy-start.1
  42.0 21.9 %copy-start.2 = (bf16[512,3,128]{2,1,0:T(4,128)(2,1)S(1)}, bf16[512,3,128]{2,1,0:T(4,128)(2,1)}, u32[]{:S(2)}) copy-start(bf16[512,3,128]{2,1,0:T(4,128)(2,1)} %copy.18) | copy-start | bytes 1179652
  45.3 26.5 %copy-start.5 = (bf16[64,64,64]{2,1,0:T(8,128)(2,1)S(1)}, bf16[64,64,64]{2,1,0:T(8,128)(2,1)}, u32[]{:S(2)}) copy-start(bf16[64,64,64]{2,1,0:T(8,128)(2,1)} %param.23) | copy-start | bytes 1572868
  54.8 92.6 %collective-permute-start.2 = (bf16[64,8,64]{2,1,0:T(8,128)(2,1)S(1)}, bf16[64,8,64]{2,1,0:T(8,128)(2,1)}, u32[]{:S(2)}, u32[]{:S(2)}) collective-permute-start(bf16[64,8,64]{2,1,0:T(8,128)(2,1)S(1)} %all_gather.10), channel_id=1, source_target_pairs={{0,4},{4,8},{8,12},{12,16},{16,20},{20,24},{24,28},{28,32},{32,36}... | collective-permute-start | bytes 196616 | tf_op jit(solution)/shard_map/ppermute | solution.py:18
  62.0 85.5 %collective-permute-start.3 = (bf16[64,8,64]{2,1,0:T(8,128)(2,1)S(1)}, bf16[64,8,64]{2,1,0:T(8,128)(2,1)}, u32[]{:S(2)}, u32[]{:S(2)}) collective-permute-start(bf16[64,8,64]{2,1,0:T(8,128)(2,1)S(1)} %all_gather.10), channel_id=1, source_target_pairs={{4,0},{8,4},{12,8},{16,12},{20,16},{24,20},{28,24},{32,28},{36,32}... | collective-permute-start | bytes 196616 | tf_op jit(solution)/shard_map/ppermute | solution.py:20
  66.2 95.9 %collective-permute-start = (bf16[512,11,128]{2,0,1:T(8,128)(2,1)}, bf16[512,11,128]{2,0,1:T(8,128)(2,1)}, u32[]{:S(2)}, u32[]{:S(2)}) collective-permute-start(bf16[512,11,128]{2,0,1:T(8,128)(2,1)} %copy.19), channel_id=1, source_target_pairs={{0,4},{4,8},{8,12},{12,16},{16,20},{20,24},{24,28},{28,32},{32,36}... | collective-permute-start | bytes 4325384 | tf_op jit(solution)/shard_map/ppermute | solution.py:18
  69.9 94.7 %collective-permute-start.1 = (bf16[512,11,128]{2,0,1:T(8,128)(2,1)}, bf16[512,11,128]{2,0,1:T(8,128)(2,1)}, u32[]{:S(2)}, u32[]{:S(2)}) collective-permute-start(bf16[512,11,128]{2,0,1:T(8,128)(2,1)} %copy.19), channel_id=1, source_target_pairs={{4,0},{8,4},{12,8},{16,12},{20,16},{24,20},{28,24},{32,28},{36,32}... | collective-permute-start | bytes 4325384 | tf_op jit(solution)/shard_map/ppermute | solution.py:20
  162.1 4.8 copy-start.3
  192.7 482.2 %copy-start.4 = (f32[128,8,128]{2,1,0:T(8,128)S(1)}, f32[128,8,128]{2,1,0:T(8,128)}, u32[]{:S(2)}) copy-start(f32[128,8,128]{2,1,0:T(8,128)} %fusion.34) | copy-start | bytes 1572868
Sparse Core Ops, SparseCore 0:
  9.2 29.4 all-gather.2
where the time goes:
time: 689 us; the launch traced here: 684 us
  matrix products  325 us (47%)
  local copies, waits for them, and re-layouts  140 us (20%)
  other arithmetic  87.3 us (13%)
  blocking collectives  82.3 us (12%)
  waiting for transfers between devices  20.1 us (3%)
  starting transfers between devices  14.7 us (2%)
  between operations  13.6 us (2%)
    dot_general x27, matrix products, slot_step(): jnp.einsum('tij,trj->tri', tile, source, preferred_element_type=jnp.float32)  312 us
    gather x27, local copies, waits for them, and re-layouts, slot_step(): rows = nearby[index]  94.2 us
    all_gather x1, blocking collectives, on_device(): all_top = lax.all_gather(top_moment[None], 'leaf', axis=0, tiled=True)  72.7 us
    ge x27, other arithmetic, slot_step(): valid = column >= 0  32.9 us
    concatenate x2, other arithmetic, with_halo(): jnp.concatenate([lax.ppermute(tail, axis, [(i, (i + 1) % count) for i in...  27.6 us
    all_gather x1, waiting for transfers between devices, on_device(): arrived = lax.all_gather(charges, 'sub', axis=0, tiled=True)  19.4 us
    select_n x27, other arithmetic, slot_step(): rows = nearby[index]  19 us
    sub x27, local copies, waits for them, and re-layouts, kernel_tile(): offset = targets[:, component, :, None] - sources[:, component, None, :]  18.6 us
  transfers between devices with their start and end apart: 5, of which 1 were waited for; matrix products, arithmetic and copies ran while one was open for 5% of the time, Pallas kernels for 0%

commit v1 on v0

--- a/solution.py
+++ b/solution.py
@@ -63,7 +63,21 @@
     clusters = far2_list.shape[0]
     group_boxes = transfer2.shape[0]
     start = lane * leaf_dev
-    arrived = lax.all_gather(charges, "sub", axis=0, tiled=True)
+    ways, here, turn = (lax.axis_size("sub"), lax.axis_index("sub"), charges.shape[0])
+    shape = [n * ways if d == 0 else n for d, n in enumerate(charges.shape)]
+    full = lax.dynamic_update_slice_in_dim(
+        jnp.zeros(shape, charges.dtype), charges, here * turn, axis=0
+    )
+    going_up = going_down = charges
+    for far in range(1, ways // 2 + 1):
+        going_up = lax.ppermute(going_up, "sub", [(d, (d + 1) % ways) for d in range(ways)])
+        full = lax.dynamic_update_slice_in_dim(full, going_up, (here - far) % ways * turn, axis=0)
+        if 2 * far < ways:
+            going_down = lax.ppermute(going_down, "sub", [(d, (d - 1) % ways) for d in range(ways)])
+            full = lax.dynamic_update_slice_in_dim(
+                full, going_down, (here + far) % ways * turn, axis=0
+            )
+    arrived = full
     inverse = (
         jnp.zeros((group_size,), jnp.int32).at[morton].set(jnp.arange(group_size, dtype=jnp.int32))
     )

time: 689 us -> 668 us (0.970)
  waiting for transfers between devices: 20.1 us -> 0.02 us
  between operations: 13.6 us -> 0.29 us
    all_gather x1 -> x0, waiting for transfers between devices: 19.4 us -> none  [on_device(): arrived = lax.all_gather(charges, 'sub', axis=0, tiled=True)]
  transfers between devices with their start and end apart: 5 -> 7, of which waited for: 1 -> 0; matrix products, arithmetic and copies ran while one was open for 5% -> 6% of each run, Pallas kernels for 0% -> 0%
where the time goes in v1:
time: 668 us; the launch traced here: 662 us
  matrix products  325 us (49%)
  local copies, waits for them, and re-layouts  143 us (21%)
  other arithmetic  91.3 us (14%)
  blocking collectives  83.3 us (12%)
  starting transfers between devices  18.6 us (3%)
    dot_general x27, matrix products, slot_step(): jnp.einsum('tij,trj->tri', tile, source, preferred_element_type=jnp.float32)  312 us
    gather x27, local copies, waits for them, and re-layouts, slot_step(): rows = nearby[index]  94.2 us
    all_gather x1, blocking collectives, on_device(): all_top = lax.all_gather(top_moment[None], 'leaf', axis=0, tiled=True)  74 us
    ge x27, other arithmetic, slot_step(): valid = column >= 0  34.5 us
    concatenate x2, other arithmetic, with_halo(): jnp.concatenate([lax.ppermute(tail, axis, [(i, (i + 1) % count) for i in...  27.3 us
    select_n x27, other arithmetic, slot_step(): rows = nearby[index]  19 us
    sub x27, local copies, waits for them, and re-layouts, kernel_tile(): offset = targets[:, component, :, None] - sources[:, component, None, :]  18.5 us
  transfers between devices with their start and end apart: 7, of which 0 were waited for; matrix products, arithmetic and copies ran while one was open for 6% of the time, Pallas kernels for 0%

profile of v1, /device:TPU:1, one launch (start us, length us, event | category | flops | bytes accessed | tf_op | source)
XLA Modules:
  0.0 662.4 jit_solution(1097964356635547423)
XLA Ops:
  28.2 9.3 %all_gather.6 = bf16[64,8,64]{2,1,0:T(8,128)(2,1)S(1)} all-gather(bf16[16,8,64]{2,1,0:T(8,128)(2,1)S(1)} %fusion.10), channel_id=1, replica_groups=mesh['leaf'=64,'sub'=4] {'sub'}, dimensions={0}, use_global_device_ids=true | all-gather | bytes 81920 | tf_op jit(solution)/shard_map/all_gather | solution.py:102
  37.6 7.4 %collective-permute-start.5 = (bf16[64,8,64]{2,1,0:T(8,128)(2,1)S(1)}, bf16[64,8,64]{2,1,0:T(8,128)(2,1)}, u32[]{:S(2)}, u32[]{:S(2)}) collective-permute-start(bf16[64,8,64]{2,1,0:T(8,128)(2,1)S(1)} %all_gather.6), channel_id=1, source_target_pairs={{0,4},{4,8},{8,12},{12,16},{16,20},{20,24},{24,28},{28,32},{32,36}... | collective-permute-start | bytes 196616 | tf_op jit(solution)/shard_map/ppermute | solution.py:18
  55.1 74.0 %all-gather = bf16[512,64]{1,0:T(8,128)(2,1)} all-gather(bf16[8,64]{1,0:T(8,128)(2,1)S(1)} %fusion.12), channel_id=2, replica_groups=mesh['leaf'=64,'sub'=4] {'leaf'}, dimensions={0}, use_global_device_ids=true | all-gather | bytes 66560 | tf_op jit(solution)/shard_map/all_gather | solution.py:106
  151.2 25.5 %pad_maximum_fusion = bf16[1536,11,128]{2,1,0:T(8,128)(2,1)} fusion(bf16[512,11,128]{2,1,0:T(8,128)(2,1)S(1)} %copy.22, bf16[512,8,128]{2,1,0:T(8,128)(2,1)S(1)} %broadcast_select_fusion, bf16[512,3,128]{2,1,0:T(4,128)(2,1)S(1)} %copy-done.3, bf16[512,11,128]{2,1,0:T(8,128)(2,1)S(1)} %copy.21), kind=kLoop, calls=%fused_computation.23 | loop fusion | flops 17301504 | bytes 8650752 | tf_op jit(solution)/shard_map/concatenate | solution.py:16
  176.8 483.7 %while.11 = (s32[]{:T(128)}, f32[128,8,128]{2,1,0:T(8,128)}, s32[27,128]{1,0:T(8,128)}, s32[]{:T(128)}, bf16[1536,11,128]{2,1,0:T(8,128)(2,1)}, /*index=5*/f32[128,3,128]{2,0,1:T(8,128)S(1)}, s32[]{:T(128)}, s32[]{:T(128)}) while((s32[]{:T(128)}, f32[128,8,128]{2,1,0:T(8,128)}, s32[27,128]{1,0:T(8,128)}, s32[]{:T(128)}, ...), condition=%wide.region_2.3_spmd.clone, body=%wide.region_1.2_spmd.clone.sunk | while | flops 57067264 | bytes 3513195 | solution.py:133
  183.2 11.5 %fusion.50 = f32[128,8,128]{2,1,0:T(8,128)} fusion(f32[128,128]{1,0:T(8,128)S(1)} %bitcast.93, f32[128,128]{1,0:T(8,128)} %get-tuple-element.121, f32[128,128]{1,0:T(8,128)S(1)} %bitcast.94, f32[128,128]{1,0:T(8,128)} %get-tuple-element.123, f32[128,128]{1,0:T(8,128)S(1)} %bitcast.92, f32[128,128]{1,0:T(8,128)} %get-tuple-element.125, ...), kind=kOutput, calls=%fused_computation.7.clone.1 | convolution fusion | flops 57016320 | bytes 1704065 | tf_op jit(solution)/shard_map/while/body/eval_jaxpr/tij,trj->tri/dot_general | solution.py:129
  201.0 11.6 %fusion.50 = f32[128,8,128]{2,1,0:T(8,128)} fusion(f32[128,128]{1,0:T(8,128)S(1)} %bitcast.93, f32[128,128]{1,0:T(8,128)} %get-tuple-element.121, f32[128,128]{1,0:T(8,128)S(1)} %bitcast.94, f32[128,128]{1,0:T(8,128)} %get-tuple-element.123, f32[128,128]{1,0:T(8,128)S(1)} %bitcast.92, f32[128,128]{1,0:T(8,128)} %get-tuple-element.125, ...), kind=kOutput, calls=%fused_computation.7.clone.1 | convolution fusion | flops 57016320 | bytes 1704065 | tf_op jit(solution)/shard_map/while/body/eval_jaxpr/tij,trj->tri/dot_general | solution.py:129
  218.9 11.6 %fusion.50 = f32[128,8,128]{2,1,0:T(8,128)} fusion(f32[128,128]{1,0:T(8,128)S(1)} %bitcast.93, f32[128,128]{1,0:T(8,128)} %get-tuple-element.121, f32[128,128]{1,0:T(8,128)S(1)} %bitcast.94, f32[128,128]{1,0:T(8,128)} %get-tuple-element.123, f32[128,128]{1,0:T(8,128)S(1)} %bitcast.92, f32[128,128]{1,0:T(8,128)} %get-tuple-element.125, ...), kind=kOutput, calls=%fused_computation.7.clone.1 | convolution fusion | flops 57016320 | bytes 1704065 | tf_op jit(solution)/shard_map/while/body/eval_jaxpr/tij,trj->tri/dot_general | solution.py:129
  236.9 11.6 %fusion.50 = f32[128,8,128]{2,1,0:T(8,128)} fusion(f32[128,128]{1,0:T(8,128)S(1)} %bitcast.93, f32[128,128]{1,0:T(8,128)} %get-tuple-element.121, f32[128,128]{1,0:T(8,128)S(1)} %bitcast.94, f32[128,128]{1,0:T(8,128)} %get-tuple-element.123, f32[128,128]{1,0:T(8,128)S(1)} %bitcast.92, f32[128,128]{1,0:T(8,128)} %get-tuple-element.125, ...), kind=kOutput, calls=%fused_computation.7.clone.1 | convolution fusion | flops 57016320 | bytes 1704065 | tf_op jit(solution)/shard_map/while/body/eval_jaxpr/tij,trj->tri/dot_general | solution.py:129
  254.8 11.6 %fusion.50 = f32[128,8,128]{2,1,0:T(8,128)} fusion(f32[128,128]{1,0:T(8,128)S(1)} %bitcast.93, f32[128,128]{1,0:T(8,128)} %get-tuple-element.121, f32[128,128]{1,0:T(8,128)S(1)} %bitcast.94, f32[128,128]{1,0:T(8,128)} %get-tuple-element.123, f32[128,128]{1,0:T(8,128)S(1)} %bitcast.92, f32[128,128]{1,0:T(8,128)} %get-tuple-element.125, ...), kind=kOutput, calls=%fused_computation.7.clone.1 | convolution fusion | flops 57016320 | bytes 1704065 | tf_op jit(solution)/shard_map/while/body/eval_jaxpr/tij,trj->tri/dot_general | solution.py:129
  272.7 11.6 %fusion.50 = f32[128,8,128]{2,1,0:T(8,128)} fusion(f32[128,128]{1,0:T(8,128)S(1)} %bitcast.93, f32[128,128]{1,0:T(8,128)} %get-tuple-element.121, f32[128,128]{1,0:T(8,128)S(1)} %bitcast.94, f32[128,128]{1,0:T(8,128)} %get-tuple-element.123, f32[128,128]{1,0:T(8,128)S(1)} %bitcast.92, f32[128,128]{1,0:T(8,128)} %get-tuple-element.125, ...), kind=kOutput, calls=%fused_computation.7.clone.1 | convolution fusion | flops 57016320 | bytes 1704065 | tf_op jit(solution)/shard_map/while/body/eval_jaxpr/tij,trj->tri/dot_general | solution.py:129
  290.6 11.6 %fusion.50 = f32[128,8,128]{2,1,0:T(8,128)} fusion(f32[128,128]{1,0:T(8,128)S(1)} %bitcast.93, f32[128,128]{1,0:T(8,128)} %get-tuple-element.121, f32[128,128]{1,0:T(8,128)S(1)} %bitcast.94, f32[128,128]{1,0:T(8,128)} %get-tuple-element.123, f32[128,128]{1,0:T(8,128)S(1)} %bitcast.92, f32[128,128]{1,0:T(8,128)} %get-tuple-element.125, ...), kind=kOutput, calls=%fused_computation.7.clone.1 | convolution fusion | flops 57016320 | bytes 1704065 | tf_op jit(solution)/shard_map/while/body/eval_jaxpr/tij,trj->tri/dot_general | solution.py:129
  308.5 11.6 %fusion.50 = f32[128,8,128]{2,1,0:T(8,128)} fusion(f32[128,128]{1,0:T(8,128)S(1)} %bitcast.93, f32[128,128]{1,0:T(8,128)} %get-tuple-element.121, f32[128,128]{1,0:T(8,128)S(1)} %bitcast.94, f32[128,128]{1,0:T(8,128)} %get-tuple-element.123, f32[128,128]{1,0:T(8,128)S(1)} %bitcast.92, f32[128,128]{1,0:T(8,128)} %get-tuple-element.125, ...), kind=kOutput, calls=%fused_computation.7.clone.1 | convolution fusion | flops 57016320 | bytes 1704065 | tf_op jit(solution)/shard_map/while/body/eval_jaxpr/tij,trj->tri/dot_general | solution.py:129
  326.4 11.6 %fusion.50 = f32[128,8,128]{2,1,0:T(8,128)} fusion(f32[128,128]{1,0:T(8,128)S(1)} %bitcast.93, f32[128,128]{1,0:T(8,128)} %get-tuple-element.121, f32[128,128]{1,0:T(8,128)S(1)} %bitcast.94, f32[128,128]{1,0:T(8,128)} %get-tuple-element.123, f32[128,128]{1,0:T(8,128)S(1)} %bitcast.92, f32[128,128]{1,0:T(8,128)} %get-tuple-element.125, ...), kind=kOutput, calls=%fused_computation.7.clone.1 | convolution fusion | flops 57016320 | bytes 1704065 | tf_op jit(solution)/shard_map/while/body/eval_jaxpr/tij,trj->tri/dot_general | solution.py:129
  344.4 11.6 %fusion.50 = f32[128,8,128]{2,1,0:T(8,128)} fusion(f32[128,128]{1,0:T(8,128)S(1)} %bitcast.93, f32[128,128]{1,0:T(8,128)} %get-tuple-element.121, f32[128,128]{1,0:T(8,128)S(1)} %bitcast.94, f32[128,128]{1,0:T(8,128)} %get-tuple-element.123, f32[128,128]{1,0:T(8,128)S(1)} %bitcast.92, f32[128,128]{1,0:T(8,128)} %get-tuple-element.125, ...), kind=kOutput, calls=%fused_computation.7.clone.1 | convolution fusion | flops 57016320 | bytes 1704065 | tf_op jit(solution)/shard_map/while/body/eval_jaxpr/tij,trj->tri/dot_general | solution.py:129
  362.3 11.6 %fusion.50 = f32[128,8,128]{2,1,0:T(8,128)} fusion(f32[128,128]{1,0:T(8,128)S(1)} %bitcast.93, f32[128,128]{1,0:T(8,128)} %get-tuple-element.121, f32[128,128]{1,0:T(8,128)S(1)} %bitcast.94, f32[128,128]{1,0:T(8,128)} %get-tuple-element.123, f32[128,128]{1,0:T(8,128)S(1)} %bitcast.92, f32[128,128]{1,0:T(8,128)} %get-tuple-element.125, ...), kind=kOutput, calls=%fused_computation.7.clone.1 | convolution fusion | flops 57016320 | bytes 1704065 | tf_op jit(solution)/shard_map/while/body/eval_jaxpr/tij,trj->tri/dot_general | solution.py:129
  380.2 11.6 %fusion.50 = f32[128,8,128]{2,1,0:T(8,128)} fusion(f32[128,128]{1,0:T(8,128)S(1)} %bitcast.93, f32[128,128]{1,0:T(8,128)} %get-tuple-element.121, f32[128,128]{1,0:T(8,128)S(1)} %bitcast.94, f32[128,128]{1,0:T(8,128)} %get-tuple-element.123, f32[128,128]{1,0:T(8,128)S(1)} %bitcast.92, f32[128,128]{1,0:T(8,128)} %get-tuple-element.125, ...), kind=kOutput, calls=%fused_computation.7.clone.1 | convolution fusion | flops 57016320 | bytes 1704065 | tf_op jit(solution)/shard_map/while/body/eval_jaxpr/tij,trj->tri/dot_general | solution.py:129
  398.1 11.6 %fusion.50 = f32[128,8,128]{2,1,0:T(8,128)} fusion(f32[128,128]{1,0:T(8,128)S(1)} %bitcast.93, f32[128,128]{1,0:T(8,128)} %get-tuple-element.121, f32[128,128]{1,0:T(8,128)S(1)} %bitcast.94, f32[128,128]{1,0:T(8,128)} %get-tuple-element.123, f32[128,128]{1,0:T(8,128)S(1)} %bitcast.92, f32[128,128]{1,0:T(8,128)} %get-tuple-element.125, ...), kind=kOutput, calls=%fused_computation.7.clone.1 | convolution fusion | flops 57016320 | bytes 1704065 | tf_op jit(solution)/shard_map/while/body/eval_jaxpr/tij,trj->tri/dot_general | solution.py:129
  416.0 11.6 %fusion.50 = f32[128,8,128]{2,1,0:T(8,128)} fusion(f32[128,128]{1,0:T(8,128)S(1)} %bitcast.93, f32[128,128]{1,0:T(8,128)} %get-tuple-element.121, f32[128,128]{1,0:T(8,128)S(1)} %bitcast.94, f32[128,128]{1,0:T(8,128)} %get-tuple-element.123, f32[128,128]{1,0:T(8,128)S(1)} %bitcast.92, f32[128,128]{1,0:T(8,128)} %get-tuple-element.125, ...), kind=kOutput, calls=%fused_computation.7.clone.1 | convolution fusion | flops 57016320 | bytes 1704065 | tf_op jit(solution)/shard_map/while/body/eval_jaxpr/tij,trj->tri/dot_general | solution.py:129
  433.9 11.6 %fusion.50 = f32[128,8,128]{2,1,0:T(8,128)} fusion(f32[128,128]{1,0:T(8,128)S(1)} %bitcast.93, f32[128,128]{1,0:T(8,128)} %get-tuple-element.121, f32[128,128]{1,0:T(8,128)S(1)} %bitcast.94, f32[128,128]{1,0:T(8,128)} %get-tuple-element.123, f32[128,128]{1,0:T(8,128)S(1)} %bitcast.92, f32[128,128]{1,0:T(8,128)} %get-tuple-element.125, ...), kind=kOutput, calls=%fused_computation.7.clone.1 | convolution fusion | flops 57016320 | bytes 1704065 | tf_op jit(solution)/shard_map/while/body/eval_jaxpr/tij,trj->tri/dot_general | solution.py:129
  451.9 11.6 %fusion.50 = f32[128,8,128]{2,1,0:T(8,128)} fusion(f32[128,128]{1,0:T(8,128)S(1)} %bitcast.93, f32[128,128]{1,0:T(8,128)} %get-tuple-element.121, f32[128,128]{1,0:T(8,128)S(1)} %bitcast.94, f32[128,128]{1,0:T(8,128)} %get-tuple-element.123, f32[128,128]{1,0:T(8,128)S(1)} %bitcast.92, f32[128,128]{1,0:T(8,128)} %get-tuple-element.125, ...), kind=kOutput, calls=%fused_computation.7.clone.1 | convolution fusion | flops 57016320 | bytes 1704065 | tf_op jit(solution)/shard_map/while/body/eval_jaxpr/tij,trj->tri/dot_general | solution.py:129
  469.8 11.6 %fusion.50 = f32[128,8,128]{2,1,0:T(8,128)} fusion(f32[128,128]{1,0:T(8,128)S(1)} %bitcast.93, f32[128,128]{1,0:T(8,128)} %get-tuple-element.121, f32[128,128]{1,0:T(8,128)S(1)} %bitcast.94, f32[128,128]{1,0:T(8,128)} %get-tuple-element.123, f32[128,128]{1,0:T(8,128)S(1)} %bitcast.92, f32[128,128]{1,0:T(8,128)} %get-tuple-element.125, ...), kind=kOutput, calls=%fused_computation.7.clone.1 | convolution fusion | flops 57016320 | bytes 1704065 | tf_op jit(solution)/shard_map/while/body/eval_jaxpr/tij,trj->tri/dot_general | solution.py:129
  487.7 11.6 %fusion.50 = f32[128,8,128]{2,1,0:T(8,128)} fusion(f32[128,128]{1,0:T(8,128)S(1)} %bitcast.93, f32[128,128]{1,0:T(8,128)} %get-tuple-element.121, f32[128,128]{1,0:T(8,128)S(1)} %bitcast.94, f32[128,128]{1,0:T(8,128)} %get-tuple-element.123, f32[128,128]{1,0:T(8,128)S(1)} %bitcast.92, f32[128,128]{1,0:T(8,128)} %get-tuple-element.125, ...), kind=kOutput, calls=%fused_computation.7.clone.1 | convolution fusion | flops 57016320 | bytes 1704065 | tf_op jit(solution)/shard_map/while/body/eval_jaxpr/tij,trj->tri/dot_general | solution.py:129
  505.6 11.6 %fusion.50 = f32[128,8,128]{2,1,0:T(8,128)} fusion(f32[128,128]{1,0:T(8,128)S(1)} %bitcast.93, f32[128,128]{1,0:T(8,128)} %get-tuple-element.121, f32[128,128]{1,0:T(8,128)S(1)} %bitcast.94, f32[128,128]{1,0:T(8,128)} %get-tuple-element.123, f32[128,128]{1,0:T(8,128)S(1)} %bitcast.92, f32[128,128]{1,0:T(8,128)} %get-tuple-element.125, ...), kind=kOutput, calls=%fused_computation.7.clone.1 | convolution fusion | flops 57016320 | bytes 1704065 | tf_op jit(solution)/shard_map/while/body/eval_jaxpr/tij,trj->tri/dot_general | solution.py:129
  523.5 11.6 %fusion.50 = f32[128,8,128]{2,1,0:T(8,128)} fusion(f32[128,128]{1,0:T(8,128)S(1)} %bitcast.93, f32[128,128]{1,0:T(8,128)} %get-tuple-element.121, f32[128,128]{1,0:T(8,128)S(1)} %bitcast.94, f32[128,128]{1,0:T(8,128)} %get-tuple-element.123, f32[128,128]{1,0:T(8,128)S(1)} %bitcast.92, f32[128,128]{1,0:T(8,128)} %get-tuple-element.125, ...), kind=kOutput, calls=%fused_computation.7.clone.1 | convolution fusion | flops 57016320 | bytes 1704065 | tf_op jit(solution)/shard_map/while/body/eval_jaxpr/tij,trj->tri/dot_general | solution.py:129
  541.4 11.6 %fusion.50 = f32[128,8,128]{2,1,0:T(8,128)} fusion(f32[128,128]{1,0:T(8,128)S(1)} %bitcast.93, f32[128,128]{1,0:T(8,128)} %get-tuple-element.121, f32[128,128]{1,0:T(8,128)S(1)} %bitcast.94, f32[128,128]{1,0:T(8,128)} %get-tuple-element.123, f32[128,128]{1,0:T(8,128)S(1)} %bitcast.92, f32[128,128]{1,0:T(8,128)} %get-tuple-element.125, ...), kind=kOutput, calls=%fused_computation.7.clone.1 | convolution fusion | flops 57016320 | bytes 1704065 | tf_op jit(solution)/shard_map/while/body/eval_jaxpr/tij,trj->tri/dot_general | solution.py:129
  559.4 11.6 %fusion.50 = f32[128,8,128]{2,1,0:T(8,128)} fusion(f32[128,128]{1,0:T(8,128)S(1)} %bitcast.93, f32[128,128]{1,0:T(8,128)} %get-tuple-element.121, f32[128,128]{1,0:T(8,128)S(1)} %bitcast.94, f32[128,128]{1,0:T(8,128)} %get-tuple-element.123, f32[128,128]{1,0:T(8,128)S(1)} %bitcast.92, f32[128,128]{1,0:T(8,128)} %get-tuple-element.125, ...), kind=kOutput, calls=%fused_computation.7.clone.1 | convolution fusion | flops 57016320 | bytes 1704065 | tf_op jit(solution)/shard_map/while/body/eval_jaxpr/tij,trj->tri/dot_general | solution.py:129
  577.3 11.6 %fusion.50 = f32[128,8,128]{2,1,0:T(8,128)} fusion(f32[128,128]{1,0:T(8,128)S(1)} %bitcast.93, f32[128,128]{1,0:T(8,128)} %get-tuple-element.121, f32[128,128]{1,0:T(8,128)S(1)} %bitcast.94, f32[128,128]{1,0:T(8,128)} %get-tuple-element.123, f32[128,128]{1,0:T(8,128)S(1)} %bitcast.92, f32[128,128]{1,0:T(8,128)} %get-tuple-element.125, ...), kind=kOutput, calls=%fused_computation.7.clone.1 | convolution fusion | flops 57016320 | bytes 1704065 | tf_op jit(solution)/shard_map/while/body/eval_jaxpr/tij,trj->tri/dot_general | solution.py:129
  595.2 11.6 %fusion.50 = f32[128,8,128]{2,1,0:T(8,128)} fusion(f32[128,128]{1,0:T(8,128)S(1)} %bitcast.93, f32[128,128]{1,0:T(8,128)} %get-tuple-element.121, f32[128,128]{1,0:T(8,128)S(1)} %bitcast.94, f32[128,128]{1,0:T(8,128)} %get-tuple-element.123, f32[128,128]{1,0:T(8,128)S(1)} %bitcast.92, f32[128,128]{1,0:T(8,128)} %get-tuple-element.125, ...), kind=kOutput, calls=%fused_computation.7.clone.1 | convolution fusion | flops 57016320 | bytes 1704065 | tf_op jit(solution)/shard_map/while/body/eval_jaxpr/tij,trj->tri/dot_general | solution.py:129
  613.1 11.6 %fusion.50 = f32[128,8,128]{2,1,0:T(8,128)} fusion(f32[128,128]{1,0:T(8,128)S(1)} %bitcast.93, f32[128,128]{1,0:T(8,128)} %get-tuple-element.121, f32[128,128]{1,0:T(8,128)S(1)} %bitcast.94, f32[128,128]{1,0:T(8,128)} %get-tuple-element.123, f32[128,128]{1,0:T(8,128)S(1)} %bitcast.92, f32[128,128]{1,0:T(8,128)} %get-tuple-element.125, ...), kind=kOutput, calls=%fused_computation.7.clone.1 | convolution fusion | flops 57016320 | bytes 1704065 | tf_op jit(solution)/shard_map/while/body/eval_jaxpr/tij,trj->tri/dot_general | solution.py:129
  631.0 11.6 %fusion.50 = f32[128,8,128]{2,1,0:T(8,128)} fusion(f32[128,128]{1,0:T(8,128)S(1)} %bitcast.93, f32[128,128]{1,0:T(8,128)} %get-tuple-element.121, f32[128,128]{1,0:T(8,128)S(1)} %bitcast.94, f32[128,128]{1,0:T(8,128)} %get-tuple-element.123, f32[128,128]{1,0:T(8,128)S(1)} %bitcast.92, f32[128,128]{1,0:T(8,128)} %get-tuple-element.125, ...), kind=kOutput, calls=%fused_computation.7.clone.1 | convolution fusion | flops 57016320 | bytes 1704065 | tf_op jit(solution)/shard_map/while/body/eval_jaxpr/tij,trj->tri/dot_general | solution.py:129
  648.9 11.6 %fusion.50 = f32[128,8,128]{2,1,0:T(8,128)} fusion(f32[128,128]{1,0:T(8,128)S(1)} %bitcast.93, f32[128,128]{1,0:T(8,128)} %get-tuple-element.121, f32[128,128]{1,0:T(8,128)S(1)} %bitcast.94, f32[128,128]{1,0:T(8,128)} %get-tuple-element.123, f32[128,128]{1,0:T(8,128)S(1)} %bitcast.92, f32[128,128]{1,0:T(8,128)} %get-tuple-element.125, ...), kind=kOutput, calls=%fused_computation.7.clone.1 | convolution fusion | flops 57016320 | bytes 1704065 | tf_op jit(solution)/shard_map/while/body/eval_jaxpr/tij,trj->tri/dot_general | solution.py:129
  (254 shorter events, 233.0 us)
Async XLA Ops:
  0.0 26.6 %copy-start = (bf16[128,64,128]{2,1,0:T(8,128)(2,1)S(1)}, bf16[128,64,128]{2,1,0:T(8,128)(2,1)}, u32[]{:S(2)}) copy-start(bf16[128,64,128]{2,1,0:T(8,128)(2,1)} %param.19) | copy-start | bytes 6291460
  0.0 12.5 %collective-permute-start = (bf16[128,8,128]{2,1,0:T(8,128)(2,1)}, bf16[128,8,128]{2,1,0:T(8,128)(2,1)}, u32[]{:S(2)}, u32[]{:S(2)}) collective-permute-start(bf16[128,8,128]{2,1,0:T(8,128)(2,1)} %param.15), channel_id=1, source_target_pairs={{0,1},{1,2},{2,3},{3,0},{4,5},{5,6},{6,7},{7,4},{8,9},{9,10},{10,1... | collective-permute-start | bytes 786440 | tf_op jit(solution)/shard_map/ppermute | solution.py:73
  2.1 18.4 %collective-permute-start.1 = (bf16[128,8,128]{2,1,0:T(8,128)(2,1)}, bf16[128,8,128]{2,1,0:T(8,128)(2,1)}, u32[]{:S(2)}, u32[]{:S(2)}) collective-permute-start(bf16[128,8,128]{2,1,0:T(8,128)(2,1)} %param.15), channel_id=1, source_target_pairs={{0,3},{1,0},{2,1},{3,2},{4,7},{5,4},{6,5},{7,6},{8,11},{9,8},{10,9... | collective-permute-start | bytes 786440 | tf_op jit(solution)/shard_map/ppermute | solution.py:76
  12.5 9.0 %collective-permute-start.2 = (bf16[128,8,128]{2,1,0:T(8,128)(2,1)}, bf16[128,8,128]{2,1,0:T(8,128)(2,1)}, u32[]{:S(2)}, u32[]{:S(2)}) collective-permute-start(bf16[128,8,128]{2,1,0:T(8,128)(2,1)} %collective-permute-done), channel_id=1, source_target_pairs={{0,1},{1,2},{2,3},{3,0},{4,5},{5,6},{6,7},{7,4},{8,9},{9,10},{10,1... | collective-permute-start | bytes 786440 | tf_op jit(solution)/shard_map/ppermute | solution.py:73
  24.9 2.9 copy-start.1
  24.9 22.1 %copy-start.2 = (bf16[512,3,128]{2,1,0:T(4,128)(2,1)S(1)}, bf16[512,3,128]{2,1,0:T(4,128)(2,1)}, u32[]{:S(2)}) copy-start(bf16[512,3,128]{2,1,0:T(4,128)(2,1)} %copy.18) | copy-start | bytes 1179652
  28.2 26.6 %copy-start.5 = (bf16[64,64,64]{2,1,0:T(8,128)(2,1)S(1)}, bf16[64,64,64]{2,1,0:T(8,128)(2,1)}, u32[]{:S(2)}) copy-start(bf16[64,64,64]{2,1,0:T(8,128)(2,1)} %param.23) | copy-start | bytes 1572868
  37.6 94.2 %collective-permute-start.5 = (bf16[64,8,64]{2,1,0:T(8,128)(2,1)S(1)}, bf16[64,8,64]{2,1,0:T(8,128)(2,1)}, u32[]{:S(2)}, u32[]{:S(2)}) collective-permute-start(bf16[64,8,64]{2,1,0:T(8,128)(2,1)S(1)} %all_gather.6), channel_id=1, source_target_pairs={{0,4},{4,8},{8,12},{12,16},{16,20},{20,24},{24,28},{28,32},{32,36}... | collective-permute-start | bytes 196616 | tf_op jit(solution)/shard_map/ppermute | solution.py:18
  45.0 86.8 %collective-permute-start.6 = (bf16[64,8,64]{2,1,0:T(8,128)(2,1)S(1)}, bf16[64,8,64]{2,1,0:T(8,128)(2,1)}, u32[]{:S(2)}, u32[]{:S(2)}) collective-permute-start(bf16[64,8,64]{2,1,0:T(8,128)(2,1)S(1)} %all_gather.6), channel_id=1, source_target_pairs={{4,0},{8,4},{12,8},{16,12},{20,16},{24,20},{28,24},{32,28},{36,32}... | collective-permute-start | bytes 196616 | tf_op jit(solution)/shard_map/ppermute | solution.py:20
  49.4 97.1 %collective-permute-start.3 = (bf16[512,11,128]{2,0,1:T(8,128)(2,1)}, bf16[512,11,128]{2,0,1:T(8,128)(2,1)}, u32[]{:S(2)}, u32[]{:S(2)}) collective-permute-start(bf16[512,11,128]{2,0,1:T(8,128)(2,1)} %copy.19), channel_id=1, source_target_pairs={{0,4},{4,8},{8,12},{12,16},{16,20},{20,24},{24,28},{28,32},{32,36}... | collective-permute-start | bytes 4325384 | tf_op jit(solution)/shard_map/ppermute | solution.py:18
  52.9 96.0 %collective-permute-start.4 = (bf16[512,11,128]{2,0,1:T(8,128)(2,1)}, bf16[512,11,128]{2,0,1:T(8,128)(2,1)}, u32[]{:S(2)}, u32[]{:S(2)}) collective-permute-start(bf16[512,11,128]{2,0,1:T(8,128)(2,1)} %copy.19), channel_id=1, source_target_pairs={{4,0},{8,4},{12,8},{16,12},{20,16},{24,20},{28,24},{32,28},{36,32}... | collective-permute-start | bytes 4325384 | tf_op jit(solution)/shard_map/ppermute | solution.py:20
  146.4 4.8 copy-start.3
  176.8 483.7 %copy-start.4 = (f32[128,8,128]{2,1,0:T(8,128)S(1)}, f32[128,8,128]{2,1,0:T(8,128)}, u32[]{:S(2)}) copy-start(f32[128,8,128]{2,1,0:T(8,128)} %fusion.34) | copy-start | bytes 1572868
